TPU v7x, 32 devices: a whole 2x2x4 slice. The times are simulated.
32 devices in a mesh: tile: 8 (over z, y), grp: 4 (over x, core).
Axes of the slice: x: 2, y: 2, z: 4, core: 2. Of those that a mesh axis runs over, the one named last changes fastest.
Arguments:
- kelvin_profile: float32 [90, 8, 256], P(None, 'tile'), may hold values from 0.5 to 1.5
- moisture_profile: float32 [90, 8, 256], P(None, 'tile'), may hold values from 0.1 to 3
- spreading_number: float32 [8, 256], P('tile'), may hold values from 0.05 to 0.24
- overhead_angle_measure: float32 [8, 256], P('tile'), may hold values from 0.2 to 1
- illuminated_mask: int32 [8, 256], P('tile'), may hold values 0 or 1
- radiating_tiles: int32 [2048, 1], P('tile'), may hold values from 0 to 7; in each aligned block of 256 rows (0 to 255, 256 to 511, ...) at most 64 rows name the same one
- cloudy_member_factors: float32 [224, 4096], P('grp', 'tile'), may hold values from 0.25 to 2
- arid_opacity_table: float32 [224, 90], P('grp'), may hold values from 0.003 to 0.2
- moisture_attenuation: float32 [224], P('grp'), may hold values from 0.003 to 0.05
- blackbody_share: float32 [224], P('grp'), may hold values from 0.3 to 3
- insolation_per_quadrature: float32 [224], P('grp'), may hold values from 0.3 to 3
Outputs:
- heating: float32 [90, 8, 256], P(None, 'tile')
- temp_next: float32 [90, 8, 256], P(None, 'tile')
- vapour_next: float32 [90, 8, 256], P(None, 'tile')
Inputs may be any that keep to these rules, and one draw needn't show every extreme that they name: `radiating_tiles`: among the columns of one tile no owner is named more than 64 times, a bound that some block reaches.
All inputs are finite; a program needn't handle non-finite values. No bound on the sum of `illuminated_mask` on one device may be relied on, other than what follows from the above.
Results may differ from a plain program's by a relative error of at most 0.00025.
Values sent between devices are 32-bit elements; how exact they have to be, the bound alone decides.
No kernel may reach another device: no remote copies, remote signals or barrier semaphores. Data moves between devices by JAX's collectives and lax.ppermute only.
A program may use at most 64 MiB of HBM per device.

v0:
```python
import functools
import math

import jax
import jax.numpy as jnp
from jax import lax
from jax.experimental import pallas as pl
from jax.experimental.pallas import tpu as pltpu
from jax.sharding import PartitionSpec as P


LOG2E = math.log2(math.e)
VM = pl.BlockSpec(memory_space=pltpu.VMEM)
FAR = pl.BlockSpec(memory_space=pltpu.HBM)


def kernel_call(body, outs, scratch=(), in_specs=None, out_specs=None, aliases=None, flops=1 << 22):
    return pl.pallas_call(
        body,
        out_shape=[o if hasattr(o, "dtype") else jax.ShapeDtypeStruct(o, jnp.float32) for o in outs],
        out_specs=out_specs or [VM] * len(outs),
        scratch_shapes=list(scratch),
        input_output_aliases=aliases or {},
        compiler_params=pltpu.CompilerParams(vmem_limit_bytes=24 << 20),
        cost_estimate=pl.CostEstimate(flops=flops, bytes_accessed=1 << 21, transcendentals=0),
        **({} if in_specs is None else {"in_specs": in_specs}),
    )


def split3(x):
    high = x.astype(jnp.bfloat16)
    rest = x - high.astype(jnp.float32)
    middle = rest.astype(jnp.bfloat16)
    low = (rest - middle.astype(jnp.float32)).astype(jnp.bfloat16)
    return high, middle, low


def column_of(row):
    n = row.shape[1]
    r = lax.broadcasted_iota(jnp.int32, (n, n), 0)
    c = lax.broadcasted_iota(jnp.int32, (n, n), 1)
    return jnp.sum(jnp.where(r == c, jnp.broadcast_to(row, (n, n)), 0.0), axis=1, keepdims=True)


def around(v):
    width = v.shape[1]
    return pltpu.roll(v, width - 1, 1) + pltpu.roll(v, 1, 1) - 4.0 * v


def pack_kernel(cap, packed, kept, *refs):
    n_in = kept + 3 + packed
    given, rest = refs[:n_in], refs[n_in:]
    outs, scratch, sems = rest[: 1 + packed + kept], rest[1 + packed + kept : -1], rest[-1]
    scratch, spare = scratch[: 3 + packed], scratch[3 + packed :]
    targets = tuple(scratch) + tuple(outs[1 + packed :])
    copies = [pltpu.make_async_copy(g, t, sems.at[i]) for i, (g, t) in enumerate(zip(given, targets))]
    for copy in copies:
        copy.start()
    fields = outs[0]
    if packed:
        factors, blocks = scratch[0], spare[0]
        tiles, rows, _ = blocks.shape
        top = factors.shape[0] - rows
        lane = lax.broadcasted_iota(jnp.int32, (rows, 2 * cap), 1)
        copies[0].wait()
        for pair in range(tiles // 2):
            first = factors[0:rows, pair * 2 * cap : (pair + 1) * 2 * cap]
            second = factors[top : top + rows, pair * 2 * cap : (pair + 1) * 2 * cap]
            blocks[2 * pair] = jnp.where(lane < cap, first, pltpu.roll(second, cap, 1))
            blocks[2 * pair + 1] = jnp.where(lane < cap, pltpu.roll(first, cap, 1), second)
        parts = [pl.ds(p * (tiles // 4), tiles // 4) for p in range(4)]
        sending = [pltpu.make_async_copy(blocks.at[p], outs[1].at[p], sems.at[n_in + i]) for i, p in enumerate(parts)]
        for copy in sending:
            copy.start()
    kelvin, moisture, spread = scratch[packed:]
    for copy in copies[packed : packed + 3]:
        copy.wait()
    levels = kelvin.shape[0]
    for l in range(levels):
        fields[l : l + 1, :] = kelvin[l]
        fields[levels + l : levels + l + 1, :] = moisture[l]
    fields[2 * levels : 2 * levels + 1, :] = spread[...]
    left = fields.shape[0] - 2 * levels - 1
    if left:
        fields[2 * levels + 1 :, :] = jnp.zeros((left, fields.shape[1]), jnp.float32)
    for copy in copies[packed + 3 :]:
        copy.wait()
    if packed:
        for copy in sending:
            copy.wait()


def prepare_kernel(cap, tiles, levels, fields, near, *refs):
    given, (slot, dry, base, part, inverse, marker), rest = refs[:7], refs[7:13], refs[13:]
    targets, sems = rest[:-1], rest[-1]
    _, _, _, owners, arid, angle, lit = targets
    copies = [pltpu.make_async_copy(g, t, sems.at[i]) for i, (g, t) in enumerate(zip(given, targets))]
    for copy in copies:
        copy.start()
    f = fields[...]
    spread = fields[2 * levels : 2 * levels + 1, :]
    first = f + spread * around(f)
    other = near[...]
    v = spread * other
    side = v + spread * (around(v) + other + near[2 * levels : 2 * levels + 1, :] * (f + around(other)))
    part[...] = side
    base[...] = first + spread * around(first) + side
    for copy in copies:
        copy.wait()
    inverse[...] = 1.0 / angle[...]
    marker[...] = angle[...] * lit[...].astype(jnp.float32)
    columns = owners.shape[1]
    gpoints = arid.shape[0]
    owner = owners[...]
    matches = lax.broadcasted_iota(jnp.int32, (tiles, columns), 0) == owner
    member = matches.astype(jnp.float32)
    r = lax.broadcasted_iota(jnp.int32, (columns, columns), 0)
    c = lax.broadcasted_iota(jnp.int32, (columns, columns), 1)
    earlier = (r < c).astype(jnp.float32).astype(jnp.bfloat16)
    counts = jnp.dot(member.astype(jnp.bfloat16), earlier, preferred_element_type=jnp.float32)
    rank = jnp.sum(jnp.where(matches, counts, 0.0), axis=0, keepdims=True)
    slot[...] = owner * cap + rank.astype(jnp.int32)
    for l in range(levels):
        dry[l] = jnp.broadcast_to(arid[:, l : l + 1] * -LOG2E, (gpoints, dry.shape[2]))


def select_kernel(cap, tiles, packed, scale, homed, slot, vapour, black, solar, weights, black_column, solar_column):
    gpoints = weights.shape[0]
    if packed:
        rows = homed.shape[1]
        lane = lax.broadcasted_iota(jnp.int32, (rows, 2 * cap), 1)
        lower, upper = [], []
        for pair in range(tiles // 2):
            first, second = homed[2 * pair], homed[2 * pair + 1]
            lower.append(jnp.where(lane < cap, first, pltpu.roll(second, cap, 1)))
            upper.append(jnp.where(lane < cap, pltpu.roll(first, cap, 1), second))
        lower = jnp.concatenate(lower, axis=1)
        upper = jnp.concatenate(upper, axis=1)[2 * rows - gpoints :]
        table = jnp.concatenate([lower, upper], axis=0)
    else:
        table = homed[...]
    chosen = lax.broadcasted_iota(jnp.int32, (tiles * cap, slot.shape[1]), 0) == slot[...]
    choice = chosen.astype(jnp.float32).astype(jnp.bfloat16)
    picked = 0.0
    for part in split3(table):
        picked = picked + jnp.dot(part, choice, preferred_element_type=jnp.float32)
    weights[...] = picked * (column_of(vapour[...]) * -LOG2E)
    for row, column in ((black, black_column), (solar, solar_column)):
        column[...] = jnp.broadcast_to(column_of(row[...]) * scale, column.shape)


def side_kernel(levels, fields, near, far, base, part, share, total):
    row = slice(2 * levels, 2 * levels + 1)
    add = (fields[row, :] * near[row, :]) * far[...]
    share[...] = part[...] + add
    total[...] = base[...] + add


def spread_rows(levels, base, share, temp, wet):
    f = base[...] + share[...]
    for l in range(levels):
        temp[l] = f[l : l + 1]
        wet[l] = f[levels + l : levels + l + 1]


def tree_sum(terms):
    terms = list(terms)
    while len(terms) > 1:
        terms = [sum(terms[i + 1 : i + 2], terms[i]) for i in range(0, len(terms), 2)]
    return terms[0]


def unrolled(levels, most):
    return max(u for u in range(1, most + 1) if levels % u == 0)


UD, UU = 90, 90


def radiation_kernel(
    levels, gpoints, first, temp, wet, weights, dry, angle, lit, black, solar, part, rest, steps, sums
):
    blocks = gpoints // 8
    parity = lax.rem(lax.axis_index("grp"), 2)
    half = 1 - parity if first else parity
    at = pl.ds(pl.multiple_of(half * 128, 128), 128)
    inverse = jnp.broadcast_to(angle[:, at], (8, 128))
    marker = jnp.broadcast_to(lit[:, at], (8, 128))
    share_of = [black[8 * b : 8 * b + 8] for b in range(blocks)]
    weight = [weights[8 * b : 8 * b + 8, at] for b in range(blocks)]
    beams = tuple(solar[8 * b : 8 * b + 8] * marker for b in range(blocks))
    zero = jnp.zeros((8, 128), jnp.float32)

    def level(l):
        return pl.ds(pl.multiple_of(l * 8, 8), 8)

    def down_level(l, carry):
        down, beam = carry
        warm = jnp.broadcast_to(temp[l, :, at], (8, 128))
        moist = jnp.broadcast_to(wet[l, :, at], (8, 128))
        sums[level(l), :] = tree_sum(beam)
        new_down, new_beam = [], []
        for b in range(blocks):
            tau = dry[l, 8 * b : 8 * b + 8, :] + weight[b] * moist
            kept = jnp.exp2(tau)
            rest[l, 8 * b : 8 * b + 8, :] = kept
            steps[l, 8 * b : 8 * b + 8, :] = down[b]
            new_beam.append(beam[b] * jnp.exp2(tau * inverse))
            new_down.append(warm + kept * (down[b] - warm))
        return tuple(new_down), tuple(new_beam)

    def up_level(i, carry):
        up, below = carry
        l = levels - 1 - i
        warm = jnp.broadcast_to(temp[l, :, at], (8, 128))
        new_up, terms = [], [sums[level(l), :]]
        for b in range(blocks):
            u = warm + rest[l, 8 * b : 8 * b + 8, :] * (up[b] - warm)
            terms.append(share_of[b] * (steps[l, 8 * b : 8 * b + 8, :] - u))
            new_up.append(u)
        flux = tree_sum(terms)
        part[l] = jnp.sum(flux - below, axis=0, keepdims=True)
        return tuple(new_up), flux

    down, beam = lax.fori_loop(
        0, levels, down_level, ((zero,) * blocks, beams), unroll=unrolled(levels, UD)
    )
    floor = jnp.broadcast_to(temp[levels - 1, :, at], (8, 128))
    ground = tree_sum([s * (d - floor) for s, d in zip(share_of, down)] + list(beam))
    lax.fori_loop(0, levels, up_level, ((floor,) * blocks, ground), unroll=unrolled(levels, UU))


def first_half_kernel(
    levels, gpoints, base, share, weights, dry, angle, lit, black, solar, part, temp, wet, *scratch
):
    spread_rows(levels, base, share, temp, wet)
    radiation_kernel(levels, gpoints, True, temp, wet, weights, dry, angle, lit, black, solar, part, *scratch)


def second_half_kernel(
    levels, gpoints, temp, wet, weights, dry, angle, lit, black, solar, part, vapour, rest, steps, sums, sem
):
    copy = pltpu.make_async_copy(wet, vapour, sem)
    copy.start()
    radiation_kernel(
        levels, gpoints, False, temp, wet, weights, dry, angle, lit, black, solar, part, rest, steps, sums
    )
    copy.wait()


def finish_kernel(own_half, piece, temp, *refs):
    heating, temp_next, warm, sems = refs[-4:]
    parity = lax.rem(lax.axis_index("grp"), 2)
    half = parity if own_half else 1 - parity
    at = pl.ds(pl.multiple_of(half * 128, 128), 128)
    first = pltpu.make_async_copy(piece, heating.at[:, :, at], sems.at[0])
    first.start()
    for l in range(temp.shape[0]):
        warm[l] = temp[l, :, at] + piece[l]
    second = pltpu.make_async_copy(warm, temp_next.at[:, :, at], sems.at[1])
    second.start()
    first.wait()
    second.wait()


def on_device(
    n_tile,
    n_grp,
    kelvin,
    moisture,
    spreading_number,
    angle,
    lit,
    owners,
    factors,
    arid,
    vapour_absorption,
    black,
    solar,
):
    levels, rows, width = kelvin.shape
    gpoints, slots = factors.shape
    cap = slots // n_tile
    total_g = gpoints * n_grp
    if rows != 1 or n_grp & (n_grp - 1) or n_grp < 2 or gpoints % 8 or width != 256:
        raise ValueError("unsupported shapes")
    stacked = -(-(2 * levels + 1) // 8) * 8
    packed = 2 * cap == 128 and gpoints % 16 == 8 and n_tile % 2 == 0
    half = (gpoints + 8) // 2
    inputs = [factors] * packed + [kelvin, moisture, spreading_number]
    row = (1, gpoints)
    kept = [vapour_absorption.reshape(row), black.reshape(row), solar.reshape(row)]
    local = [owners.reshape(1, width), arid, angle, lit]
    outs = [jax.ShapeDtypeStruct((stacked, width), jnp.float32)]
    outs += [jax.ShapeDtypeStruct((n_tile, half, 128), jnp.float32)] * packed
    results = kernel_call(
        functools.partial(pack_kernel, cap, packed, 0),
        outs,
        scratch=[pltpu.VMEM(v.shape, v.dtype) for v in inputs]
        + [pltpu.VMEM((n_tile, half, 128), jnp.float32)] * packed
        + [pltpu.SemaphoreType.DMA((len(inputs) + 4 * packed,))],
        in_specs=[FAR] * len(inputs),
        out_specs=[VM] + [FAR] * packed,
    )(*(pltpu.with_memory_space_constraint(v, pltpu.HBM) for v in inputs))
    fields = results[0]
    if packed:
        homed = lax.all_to_all(results[1], "tile", split_axis=0, concat_axis=0, tiled=True)
    else:
        blocks = factors.reshape(gpoints, n_tile, cap)
        homed = lax.all_to_all(blocks, "tile", split_axis=1, concat_axis=1, tiled=True)
        homed = homed.reshape(gpoints, slots)

    def from_side(distance):
        pairs = []
        for t in range(n_tile):
            for g in range(n_grp):
                s = t - distance if g % 2 == 0 else t + distance
                if 0 <= s < n_tile:
                    pairs.append((s * n_grp + g, t * n_grp + g))
        return lax.ppermute(fields, ("tile", "grp"), pairs)

    def swapped(x, bit):
        return lax.ppermute(x, "grp", [(i, i ^ bit) for i in range(n_grp)])

    near = from_side(1)
    far = from_side(2)
    slot, dry, base, side, inverse, marker, *kept_rows = kernel_call(
        functools.partial(prepare_kernel, cap, n_tile, levels),
        [jax.ShapeDtypeStruct((1, width), jnp.int32), (levels, gpoints, 128)]
        + [(stacked, width)] * 2
        + [(1, width)] * 2
        + [row] * len(kept),
        scratch=[pltpu.VMEM(v.shape, v.dtype) for v in local]
        + [pltpu.SemaphoreType.DMA((len(kept) + len(local),))],
        in_specs=[VM] * 2 + [FAR] * (len(kept) + len(local)),
    )(fields, near, *(pltpu.with_memory_space_constraint(v, pltpu.HBM) for v in kept + local))
    weights, black_column, solar_column = kernel_call(
        functools.partial(select_kernel, cap, n_tile, packed, 1.0 / total_g),
        [(gpoints, width), (gpoints, 128), (gpoints, 128)],
    )(homed, slot, *kept_rows)
    share, mine = kernel_call(
        functools.partial(side_kernel, levels), [(stacked, width)] * 2
    )(fields, near, far, base, side)
    other = swapped(share, 1)
    tables = (weights, dry, inverse, marker, black_column, solar_column)
    work = [
        pltpu.VMEM((levels, gpoints, 128), jnp.float32),
        pltpu.VMEM((levels, gpoints, 128), jnp.float32),
        pltpu.VMEM((levels * 8, 128), jnp.float32),
    ]
    given, temp, wet = kernel_call(
        functools.partial(first_half_kernel, levels, gpoints),
        [(levels, 1, 128), (levels, 1, width), (levels, 1, width)],
        scratch=work,
    )(mine, other, *tables)
    taken = swapped(given, 1)
    part, vapour_next = kernel_call(
        functools.partial(second_half_kernel, levels, gpoints),
        [(levels, 1, 128), (levels, 1, width)],
        scratch=work + [pltpu.SemaphoreType.DMA],
        out_specs=[VM, FAR],
    )(temp, wet, *tables)
    part = part + taken
    bit = 2
    while bit < n_grp:
        part = part + swapped(part, bit)
        bit *= 2
    far_half = swapped(part, 1)
    held = [pltpu.VMEM((levels, 1, 128), jnp.float32), pltpu.SemaphoreType.DMA((2,))]
    results = ()
    for own_half, piece in ((True, part), (False, far_half)):
        results = kernel_call(
            functools.partial(finish_kernel, own_half),
            [(levels, 1, width)] * 2,
            scratch=held,
            in_specs=[VM] * 2 + [FAR] * len(results),
            out_specs=[FAR] * 2,
            aliases={2: 0, 3: 1} if results else {},
        )(piece, temp, *results)
    heating, temp_next = results
    return heating, temp_next, vapour_next


def solution(mesh):
    in_specs = (
        P(None, "tile", None),
        P(None, "tile", None),
        P("tile", None),
        P("tile", None),
        P("tile", None),
        P("tile", None),
        P("grp", "tile"),
        P("grp", None),
        P("grp"),
        P("grp"),
        P("grp"),
    )
    out_specs = (P(None, "tile", None), P(None, "tile", None), P(None, "tile", None))

    def body(*args):
        return on_device(mesh.shape["tile"], mesh.shape["grp"], *args)

    return jax.shard_map(body, mesh=mesh, in_specs=in_specs, out_specs=out_specs, check_vma=False)
```

profile of v0, /device:TPU:0, one launch (start us, length us, event | category | flops | bytes accessed | tf_op | source)
XLA Modules:
  0.0 31.6 jit_solution(13334415336416297175)
XLA Ops:
  0.6 1.7 %shard_map.130 = (f32[184,256]{1,0:T(8,128)S(1)}, f32[8,32,128]{2,1,0:T(8,128)}) custom-call(f32[56,512]{1,0:T(8,128)} %refs_0_.1, f32[90,1,256]{2,1,0:T(1,128)} %refs_1_.1, f32[90,1,256]{2,1,0:T(1,128)} %refs_2_.1, f32[1,256]{1,0:T(1,128)} %refs_3_.1), custom_call_target="tpu_custom_call" | custom-call | flops 4194304 | bytes 2097152 | tf_op jit(solution)/shard_map/pallas_call | solution.py:296
  2.4 4.9 %collective-permute-start = (f32[184,256]{1,0:T(8,128)S(1)}, f32[184,256]{1,0:T(8,128)S(1)}, u32[]{:S(2)}, u32[]{:S(2)}) collective-permute-start(f32[184,256]{1,0:T(8,128)S(1)} %get-tuple-element.28.fields), channel_id=1, source_target_pairs={{5,1},{7,3},{0,4},{9,5},{2,6},{11,7},{4,8},{13,9},{6,10},{15,11},{... | collective-permute-start | bytes 565256 | tf_op jit(solution)/shard_map/ppermute | solution.py:320
  7.3 3.5 %collective-permute-start.1 = (f32[184,256]{1,0:T(8,128)S(1)}, f32[184,256]{1,0:T(8,128)S(1)}, u32[]{:S(2)}, u32[]{:S(2)}) collective-permute-start(f32[184,256]{1,0:T(8,128)S(1)} %get-tuple-element.28.fields), channel_id=1, source_target_pairs={{9,1},{11,3},{13,5},{15,7},{0,8},{17,9},{2,10},{19,11},{4,12},{21,... | collective-permute-start | bytes 565256 | tf_op jit(solution)/shard_map/ppermute | solution.py:320
  10.8 3.9 %all-to-all-start = ((f32[8,32,128]{2,1,0:T(8,128)}), f32[8,32,128]{2,1,0:T(8,128)S(1)}, u32[]{:S(2)}, u32[]{:S(2)}) async-start(f32[8,32,128]{2,1,0:T(8,128)} %get-tuple-element.33), calls=%async_computation | async-start | bytes 262144 | tf_op jit(solution)/shard_map/all_to_all | solution.py:307
  14.6 0.0 collective-permute-done.near
  14.6 2.1 %shard_map.131 = (s32[1,256]{1,0:T(1,128)S(1)}, f32[90,56,128]{2,1,0:T(8,128)S(1)}, f32[184,256]{1,0:T(8,128)S(1)}, f32[184,256]{1,0:T(8,128)S(1)}, f32[1,256]{1...) custom-call(f32[184,256]{1,0:T(8,128)S(1)} %get-tuple-element.28.fields, ...), custom_call_target="tpu_custom_call" | custom-call | flops 4194304 | bytes 2097152 | tf_op jit(solution)/shard_map/pallas_call | solution.py:327
  16.8 0.0 collective-permute-done.1.far
  16.8 0.7 %shard_map.132 = (f32[184,256]{1,0:T(8,128)}, f32[184,256]{1,0:T(8,128)S(1)}) custom-call(f32[184,256]{1,0:T(8,128)S(1)} %get-tuple-element.28.fields, f32[184,256]{1,0:T(8,128)S(1)} %collective-permute-done.near, f32[184,256]{1,0:T(8,128)S(1)} %collective-permute-done.1.far, f32[184,256]{1,0:T(8,128)S(1)} %get-tuple-element.29.base, ...), custom_call_target="tpu_custom_call" | custom-call | flops 4194304 | bytes 2097152 | tf_op jit(solution)/shard_map/pallas_call | solution.py:341
  17.5 0.0 collective-permute-start.2
  17.5 4.5 %all-to-all-done.homed = f32[8,32,128]{2,1,0:T(8,128)S(1)} async-done(((f32[8,32,128]{2,1,0:T(8,128)}), f32[8,32,128]{2,1,0:T(8,128)S(1)}, u32[]{:S(2)}, u32[]{:S(2)}) %all-to-all-start) | async-done | bytes 131104 | tf_op jit(solution)/shard_map/all_to_all | solution.py:307
  22.0 0.3 shard_map.133
  22.3 0.0 collective-permute-done.2.share
  22.3 1.5 %shard_map.134 = (f32[90,1,128]{2,1,0:T(1,128)S(1)}, f32[90,1,256]{2,1,0:T(1,128)S(1)}, f32[90,1,256]{2,1,0:T(1,128)S(1)}) custom-call(f32[184,256]{1,0:T(8,128)S(1)} %get-tuple-element.31.base, f32[184,256]{1,0:T(8,128)S(1)} %collective-permute-done.2.share, f32[56,256]{1,0:T(8,128)S(1)} %get-tuple-element.38.weights, ...), custom_call_target="tpu_custom_call" | custom-call | flops 4194304 | bytes 2097152 | tf_op jit(solution)/shard_map/pallas_call | solution.py:351
  23.8 0.1 collective-permute-start.3
  23.9 1.5 %shard_map.135 = (f32[90,1,128]{2,1,0:T(1,128)S(1)}, f32[90,1,256]{2,1,0:T(1,128)}) custom-call(f32[90,1,256]{2,1,0:T(1,128)S(1)} %get-tuple-element.44.temp, f32[90,1,256]{2,1,0:T(1,128)S(1)} %get-tuple-element.45.wet, f32[56,256]{1,0:T(8,128)S(1)} %get-tuple-element.38.weights, f32[90,56,128]{2,1,0:T(8,128)S(1)} %get-tuple-element.39.dry, ...), custom_call_target="tpu_custom_call" | custom-call | flops 4194304 | bytes 2097152 | tf_op jit(solution)/shard_map/pallas_call | solution.py:357
  25.4 0.0 collective-permute-done.3
  25.4 0.1 add.6
  25.4 1.6 %collective-permute-start.4 = (f32[90,1,128]{2,1,0:T(1,128)S(1)}, f32[90,1,128]{2,1,0:T(1,128)S(1)}, u32[]{:S(2)}, u32[]{:S(2)}) collective-permute-start(f32[90,1,128]{2,1,0:T(1,128)S(1)} %add.6), channel_id=1, source_target_pairs={{0,2},{1,3},{2,0},{3,1},{4,6},{5,7},{6,4},{7,5},{8,10},{9,11},{10,... | collective-permute-start | bytes 138248 | tf_op jit(solution)/shard_map/ppermute | solution.py:323
  27.0 2.6 %collective-permute-done.4 = f32[90,1,128]{2,1,0:T(1,128)S(1)} collective-permute-done((f32[90,1,128]{2,1,0:T(1,128)S(1)}, f32[90,1,128]{2,1,0:T(1,128)S(1)}, u32[]{:S(2)}, u32[]{:S(2)}) %collective-permute-start.4) | collective-permute-done | bytes 46112 | tf_op jit(solution)/shard_map/ppermute | solution.py:323
  29.6 0.1 collective-permute-start.5
  29.7 0.7 %shard_map.136 = (f32[90,1,256]{2,1,0:T(1,128)}, f32[90,1,256]{2,1,0:T(1,128)}) custom-call(f32[90,1,128]{2,1,0:T(1,128)S(1)} %add.7.piece, f32[90,1,256]{2,1,0:T(1,128)S(1)} %get-tuple-element.44.temp), custom_call_target="tpu_custom_call" | custom-call | flops 4194304 | bytes 2097152 | tf_op jit(solution)/shard_map/pallas_call | solution.py:372
  30.4 0.5 %collective-permute-done.5.piece = f32[90,1,128]{2,1,0:T(1,128)S(1)} collective-permute-done((f32[90,1,128]{2,1,0:T(1,128)S(1)}, f32[90,1,128]{2,1,0:T(1,128)S(1)}, u32[]{:S(2)}, u32[]{:S(2)}) %collective-permute-start.5) | collective-permute-done | bytes 46112 | tf_op jit(solution)/shard_map/ppermute | solution.py:323
  30.9 0.7 %shard_map.137 = (f32[90,1,256]{2,1,0:T(1,128)}, f32[90,1,256]{2,1,0:T(1,128)}) custom-call(f32[90,1,128]{2,1,0:T(1,128)S(1)} %collective-permute-done.5.piece, f32[90,1,256]{2,1,0:T(1,128)S(1)} %get-tuple-element.44.temp, f32[90,1,256]{2,1,0:T(1,128)} %get-tuple-element.48.refs_0_, ...), custom_call_target="tpu_custom_call", output_to_operand_aliasing={{0}: (2, {}), {1}: (3, {})} | custom-call | flops 4194304 | bytes 2097152 | tf_op jit(solution)/shard_map/pallas_call | solution.py:372
  (1 shorter events, 0.0 us)
Async XLA Ops:
  2.4 12.3 %collective-permute-start = (f32[184,256]{1,0:T(8,128)S(1)}, f32[184,256]{1,0:T(8,128)S(1)}, u32[]{:S(2)}, u32[]{:S(2)}) collective-permute-start(f32[184,256]{1,0:T(8,128)S(1)} %get-tuple-element.28.fields), channel_id=1, source_target_pairs={{5,1},{7,3},{0,4},{9,5},{2,6},{11,7},{4,8},{13,9},{6,10},{15,11},{... | collective-permute-start | bytes 565256 | tf_op jit(solution)/shard_map/ppermute | solution.py:320
  7.3 9.5 %collective-permute-start.1 = (f32[184,256]{1,0:T(8,128)S(1)}, f32[184,256]{1,0:T(8,128)S(1)}, u32[]{:S(2)}, u32[]{:S(2)}) collective-permute-start(f32[184,256]{1,0:T(8,128)S(1)} %get-tuple-element.28.fields), channel_id=1, source_target_pairs={{9,1},{11,3},{13,5},{15,7},{0,8},{17,9},{2,10},{19,11},{4,12},{21,... | collective-permute-start | bytes 565256 | tf_op jit(solution)/shard_map/ppermute | solution.py:320
  10.8 11.2 %all-to-all-start = ((f32[8,32,128]{2,1,0:T(8,128)}), f32[8,32,128]{2,1,0:T(8,128)S(1)}, u32[]{:S(2)}, u32[]{:S(2)}) async-start(f32[8,32,128]{2,1,0:T(8,128)} %get-tuple-element.33), calls=%async_computation | async-start | bytes 262144 | tf_op jit(solution)/shard_map/all_to_all | solution.py:307
  17.5 4.8 %collective-permute-start.2 = (f32[184,256]{1,0:T(8,128)}, f32[184,256]{1,0:T(8,128)S(1)}, u32[]{:S(2)}, u32[]{:S(2)}) collective-permute-start(f32[184,256]{1,0:T(8,128)} %get-tuple-element.32), channel_id=1, source_target_pairs={{0,1},{1,0},{2,3},{3,2},{4,5},{5,4},{6,7},{7,6},{8,9},{9,8},{10,11... | collective-permute-start | bytes 565256 | tf_op jit(solution)/shard_map/ppermute | solution.py:323
  23.8 1.6 %collective-permute-start.3 = (f32[90,1,128]{2,1,0:T(1,128)S(1)}, f32[90,1,128]{2,1,0:T(1,128)S(1)}, u32[]{:S(2)}, u32[]{:S(2)}) collective-permute-start(f32[90,1,128]{2,1,0:T(1,128)S(1)} %get-tuple-element.47), channel_id=1, source_target_pairs={{0,1},{1,0},{2,3},{3,2},{4,5},{5,4},{6,7},{7,6},{8,9},{9,8},{10,11... | collective-permute-start | bytes 138248 | tf_op jit(solution)/shard_map/ppermute | solution.py:323
  25.4 4.1 %collective-permute-start.4 = (f32[90,1,128]{2,1,0:T(1,128)S(1)}, f32[90,1,128]{2,1,0:T(1,128)S(1)}, u32[]{:S(2)}, u32[]{:S(2)}) collective-permute-start(f32[90,1,128]{2,1,0:T(1,128)S(1)} %add.6), channel_id=1, source_target_pairs={{0,2},{1,3},{2,0},{3,1},{4,6},{5,7},{6,4},{7,5},{8,10},{9,11},{10,... | collective-permute-start | bytes 138248 | tf_op jit(solution)/shard_map/ppermute | solution.py:323
  29.6 1.3 %collective-permute-start.5 = (f32[90,1,128]{2,1,0:T(1,128)S(1)}, f32[90,1,128]{2,1,0:T(1,128)S(1)}, u32[]{:S(2)}, u32[]{:S(2)}) collective-permute-start(f32[90,1,128]{2,1,0:T(1,128)S(1)} %add.7.piece), channel_id=1, source_target_pairs={{0,1},{1,0},{2,3},{3,2},{4,5},{5,4},{6,7},{7,6},{8,9},{9,8},{10,11... | collective-permute-start | bytes 138248 | tf_op jit(solution)/shard_map/ppermute | solution.py:323
where the time goes:
time: 31.9 us; the launch traced here: 31.6 us
  starting transfers between devices  14 us (44%)
  Pallas kernels  9.18 us (29%)
  waiting for transfers between devices  7.6 us (24%)
  between operations  0.75 us (2%)
    ppermute x2, starting transfers between devices, from_side(): return lax.ppermute(fields, ('tile', 'grp'), pairs)  8.4 us
    all_to_all x1, waiting for transfers between devices, on_device(): lax.all_to_all(results[1], 'tile', split_axis=0, concat_axis=0, tiled=True)  4.49 us
    all_to_all x1, starting transfers between devices, on_device(): lax.all_to_all(results[1], 'tile', split_axis=0, concat_axis=0, tiled=True)  3.87 us
    ppermute x4, waiting for transfers between devices, swapped(): return lax.ppermute(x, 'grp', [(i, i ^ bit) for i in range(n_grp)])  3.1 us
    pallas_call x1, Pallas kernels, on_device(): kernel_call(functools.partial(prepare_kernel, cap, n_tile, levels), [jax....  2.11 us
    pallas_call x1, Pallas kernels, on_device(): kernel_call(functools.partial(pack_kernel, cap, packed, 0), outs, scratch...  1.71 us
    ppermute x4, starting transfers between devices, swapped(): return lax.ppermute(x, 'grp', [(i, i ^ bit) for i in range(n_grp)])  1.7 us
    pallas_call x1, Pallas kernels, on_device(): kernel_call(functools.partial(first_half_kernel, levels, gpoints), [(leve...  1.52 us
  transfers between devices with their start and end apart: 7, of which 3 were waited for; matrix products, arithmetic and copies ran while one was open for 0% of the time, Pallas kernels for 17%

commit v1 on v0

--- a/solution.py
+++ b/solution.py
@@ -68,10 +68,8 @@
             second = factors[top : top + rows, pair * 2 * cap : (pair + 1) * 2 * cap]
             blocks[2 * pair] = jnp.where(lane < cap, first, pltpu.roll(second, cap, 1))
             blocks[2 * pair + 1] = jnp.where(lane < cap, pltpu.roll(first, cap, 1), second)
-        parts = [pl.ds(p * (tiles // 4), tiles // 4) for p in range(4)]
-        sending = [pltpu.make_async_copy(blocks.at[p], outs[1].at[p], sems.at[n_in + i]) for i, p in enumerate(parts)]
-        for copy in sending:
-            copy.start()
+        sending = pltpu.make_async_copy(blocks, outs[1], sems.at[n_in])
+        sending.start()
     kelvin, moisture, spread = scratch[packed:]
     for copy in copies[packed : packed + 3]:
         copy.wait()
@@ -86,8 +84,7 @@
     for copy in copies[packed + 3 :]:
         copy.wait()
     if packed:
-        for copy in sending:
-            copy.wait()
+        sending.wait()
 
 
 def prepare_kernel(cap, tiles, levels, fields, near, *refs):
@@ -174,7 +171,7 @@
     return max(u for u in range(1, most + 1) if levels % u == 0)
 
 
-UD, UU = 90, 90
+UD, UU = 30, 90
 
 
 def radiation_kernel(
@@ -298,7 +295,7 @@
         outs,
         scratch=[pltpu.VMEM(v.shape, v.dtype) for v in inputs]
         + [pltpu.VMEM((n_tile, half, 128), jnp.float32)] * packed
-        + [pltpu.SemaphoreType.DMA((len(inputs) + 4 * packed,))],
+        + [pltpu.SemaphoreType.DMA((len(inputs) + packed,))],
         in_specs=[FAR] * len(inputs),
         out_specs=[VM] + [FAR] * packed,
     )(*(pltpu.with_memory_space_constraint(v, pltpu.HBM) for v in inputs))

time: 31.9 us -> 31.9 us (level)
  no operation moved by 1% of the time
where the time goes in v1:
time: 31.9 us; the launch traced here: 31.6 us
  starting transfers between devices  14 us (44%)
  Pallas kernels  9.17 us (29%)
  waiting for transfers between devices  7.59 us (24%)
  between operations  0.75 us (2%)
    ppermute x2, starting transfers between devices, from_side(): return lax.ppermute(fields, ('tile', 'grp'), pairs)  8.4 us
    all_to_all x1, waiting for transfers between devices, on_device(): lax.all_to_all(results[1], 'tile', split_axis=0, concat_axis=0, tiled=True)  4.49 us
    all_to_all x1, starting transfers between devices, on_device(): lax.all_to_all(results[1], 'tile', split_axis=0, concat_axis=0, tiled=True)  3.87 us
    ppermute x4, waiting for transfers between devices, swapped(): return lax.ppermute(x, 'grp', [(i, i ^ bit) for i in range(n_grp)])  3.09 us
    pallas_call x1, Pallas kernels, on_device(): kernel_call(functools.partial(prepare_kernel, cap, n_tile, levels), [jax....  2.11 us
    ppermute x4, starting transfers between devices, swapped(): return lax.ppermute(x, 'grp', [(i, i ^ bit) for i in range(n_grp)])  1.7 us
    pallas_call x1, Pallas kernels, on_device(): kernel_call(functools.partial(pack_kernel, cap, packed, 0), outs, scratch...  1.69 us
    pallas_call x1, Pallas kernels, on_device(): kernel_call(functools.partial(first_half_kernel, levels, gpoints), [(leve...  1.52 us
  transfers between devices with their start and end apart: 7, of which 3 were waited for; matrix products, arithmetic and copies ran while one was open for 0% of the time, Pallas kernels for 17%

profile of v1, /device:TPU:0, one launch (start us, length us, event | category | flops | bytes accessed | tf_op | source)
XLA Modules:
  0.0 31.6 jit_solution(6715069277176707357)
XLA Ops:
  0.6 1.7 %shard_map.130 = (f32[184,256]{1,0:T(8,128)S(1)}, f32[8,32,128]{2,1,0:T(8,128)}) custom-call(f32[56,512]{1,0:T(8,128)} %refs_0_.1, f32[90,1,256]{2,1,0:T(1,128)} %refs_1_.1, f32[90,1,256]{2,1,0:T(1,128)} %refs_2_.1, f32[1,256]{1,0:T(1,128)} %refs_3_.1), custom_call_target="tpu_custom_call" | custom-call | flops 4194304 | bytes 2097152 | tf_op jit(solution)/shard_map/pallas_call | solution.py:293
  2.3 4.9 %collective-permute-start = (f32[184,256]{1,0:T(8,128)S(1)}, f32[184,256]{1,0:T(8,128)S(1)}, u32[]{:S(2)}, u32[]{:S(2)}) collective-permute-start(f32[184,256]{1,0:T(8,128)S(1)} %get-tuple-element.28.fields), channel_id=1, source_target_pairs={{5,1},{7,3},{0,4},{9,5},{2,6},{11,7},{4,8},{13,9},{6,10},{15,11},{... | collective-permute-start | bytes 565256 | tf_op jit(solution)/shard_map/ppermute | solution.py:317
  7.2 3.5 %collective-permute-start.1 = (f32[184,256]{1,0:T(8,128)S(1)}, f32[184,256]{1,0:T(8,128)S(1)}, u32[]{:S(2)}, u32[]{:S(2)}) collective-permute-start(f32[184,256]{1,0:T(8,128)S(1)} %get-tuple-element.28.fields), channel_id=1, source_target_pairs={{9,1},{11,3},{13,5},{15,7},{0,8},{17,9},{2,10},{19,11},{4,12},{21,... | collective-permute-start | bytes 565256 | tf_op jit(solution)/shard_map/ppermute | solution.py:317
  10.7 3.9 %all-to-all-start = ((f32[8,32,128]{2,1,0:T(8,128)}), f32[8,32,128]{2,1,0:T(8,128)S(1)}, u32[]{:S(2)}, u32[]{:S(2)}) async-start(f32[8,32,128]{2,1,0:T(8,128)} %get-tuple-element.33), calls=%async_computation | async-start | bytes 262144 | tf_op jit(solution)/shard_map/all_to_all | solution.py:304
  14.6 0.0 collective-permute-done.near
  14.6 2.1 %shard_map.131 = (s32[1,256]{1,0:T(1,128)S(1)}, f32[90,56,128]{2,1,0:T(8,128)S(1)}, f32[184,256]{1,0:T(8,128)S(1)}, f32[184,256]{1,0:T(8,128)S(1)}, f32[1,256]{1...) custom-call(f32[184,256]{1,0:T(8,128)S(1)} %get-tuple-element.28.fields, ...), custom_call_target="tpu_custom_call" | custom-call | flops 4194304 | bytes 2097152 | tf_op jit(solution)/shard_map/pallas_call | solution.py:324
  16.7 0.0 collective-permute-done.1.far
  16.7 0.7 %shard_map.132 = (f32[184,256]{1,0:T(8,128)}, f32[184,256]{1,0:T(8,128)S(1)}) custom-call(f32[184,256]{1,0:T(8,128)S(1)} %get-tuple-element.28.fields, f32[184,256]{1,0:T(8,128)S(1)} %collective-permute-done.near, f32[184,256]{1,0:T(8,128)S(1)} %collective-permute-done.1.far, f32[184,256]{1,0:T(8,128)S(1)} %get-tuple-element.29.base, ...), custom_call_target="tpu_custom_call" | custom-call | flops 4194304 | bytes 2097152 | tf_op jit(solution)/shard_map/pallas_call | solution.py:338
  17.5 0.0 collective-permute-start.2
  17.5 4.5 %all-to-all-done.homed = f32[8,32,128]{2,1,0:T(8,128)S(1)} async-done(((f32[8,32,128]{2,1,0:T(8,128)}), f32[8,32,128]{2,1,0:T(8,128)S(1)}, u32[]{:S(2)}, u32[]{:S(2)}) %all-to-all-start) | async-done | bytes 131104 | tf_op jit(solution)/shard_map/all_to_all | solution.py:304
  22.0 0.3 shard_map.133
  22.2 0.0 collective-permute-done.2.share
  22.3 1.5 %shard_map.134 = (f32[90,1,128]{2,1,0:T(1,128)S(1)}, f32[90,1,256]{2,1,0:T(1,128)S(1)}, f32[90,1,256]{2,1,0:T(1,128)S(1)}) custom-call(f32[184,256]{1,0:T(8,128)S(1)} %get-tuple-element.31.base, f32[184,256]{1,0:T(8,128)S(1)} %collective-permute-done.2.share, f32[56,256]{1,0:T(8,128)S(1)} %get-tuple-element.38.weights, ...), custom_call_target="tpu_custom_call" | custom-call | flops 4194304 | bytes 2097152 | tf_op jit(solution)/shard_map/pallas_call | solution.py:348
  23.8 0.1 collective-permute-start.3
  23.9 1.5 %shard_map.135 = (f32[90,1,128]{2,1,0:T(1,128)S(1)}, f32[90,1,256]{2,1,0:T(1,128)}) custom-call(f32[90,1,256]{2,1,0:T(1,128)S(1)} %get-tuple-element.44.temp, f32[90,1,256]{2,1,0:T(1,128)S(1)} %get-tuple-element.45.wet, f32[56,256]{1,0:T(8,128)S(1)} %get-tuple-element.38.weights, f32[90,56,128]{2,1,0:T(8,128)S(1)} %get-tuple-element.39.dry, ...), custom_call_target="tpu_custom_call" | custom-call | flops 4194304 | bytes 2097152 | tf_op jit(solution)/shard_map/pallas_call | solution.py:354
  25.3 0.0 collective-permute-done.3
  25.3 0.1 add.6
  25.4 1.6 %collective-permute-start.4 = (f32[90,1,128]{2,1,0:T(1,128)S(1)}, f32[90,1,128]{2,1,0:T(1,128)S(1)}, u32[]{:S(2)}, u32[]{:S(2)}) collective-permute-start(f32[90,1,128]{2,1,0:T(1,128)S(1)} %add.6), channel_id=1, source_target_pairs={{0,2},{1,3},{2,0},{3,1},{4,6},{5,7},{6,4},{7,5},{8,10},{9,11},{10,... | collective-permute-start | bytes 138248 | tf_op jit(solution)/shard_map/ppermute | solution.py:320
  27.0 2.6 %collective-permute-done.4 = f32[90,1,128]{2,1,0:T(1,128)S(1)} collective-permute-done((f32[90,1,128]{2,1,0:T(1,128)S(1)}, f32[90,1,128]{2,1,0:T(1,128)S(1)}, u32[]{:S(2)}, u32[]{:S(2)}) %collective-permute-start.4) | collective-permute-done | bytes 46112 | tf_op jit(solution)/shard_map/ppermute | solution.py:320
  29.6 0.1 collective-permute-start.5
  29.7 0.7 %shard_map.136 = (f32[90,1,256]{2,1,0:T(1,128)}, f32[90,1,256]{2,1,0:T(1,128)}) custom-call(f32[90,1,128]{2,1,0:T(1,128)S(1)} %add.7.piece, f32[90,1,256]{2,1,0:T(1,128)S(1)} %get-tuple-element.44.temp), custom_call_target="tpu_custom_call" | custom-call | flops 4194304 | bytes 2097152 | tf_op jit(solution)/shard_map/pallas_call | solution.py:369
  30.4 0.5 %collective-permute-done.5.piece = f32[90,1,128]{2,1,0:T(1,128)S(1)} collective-permute-done((f32[90,1,128]{2,1,0:T(1,128)S(1)}, f32[90,1,128]{2,1,0:T(1,128)S(1)}, u32[]{:S(2)}, u32[]{:S(2)}) %collective-permute-start.5) | collective-permute-done | bytes 46112 | tf_op jit(solution)/shard_map/ppermute | solution.py:320
  30.9 0.7 %shard_map.137 = (f32[90,1,256]{2,1,0:T(1,128)}, f32[90,1,256]{2,1,0:T(1,128)}) custom-call(f32[90,1,128]{2,1,0:T(1,128)S(1)} %collective-permute-done.5.piece, f32[90,1,256]{2,1,0:T(1,128)S(1)} %get-tuple-element.44.temp, f32[90,1,256]{2,1,0:T(1,128)} %get-tuple-element.48.refs_0_, ...), custom_call_target="tpu_custom_call", output_to_operand_aliasing={{0}: (2, {}), {1}: (3, {})} | custom-call | flops 4194304 | bytes 2097152 | tf_op jit(solution)/shard_map/pallas_call | solution.py:369
  (1 shorter events, 0.0 us)
Async XLA Ops:
  2.3 12.3 %collective-permute-start = (f32[184,256]{1,0:T(8,128)S(1)}, f32[184,256]{1,0:T(8,128)S(1)}, u32[]{:S(2)}, u32[]{:S(2)}) collective-permute-start(f32[184,256]{1,0:T(8,128)S(1)} %get-tuple-element.28.fields), channel_id=1, source_target_pairs={{5,1},{7,3},{0,4},{9,5},{2,6},{11,7},{4,8},{13,9},{6,10},{15,11},{... | collective-permute-start | bytes 565256 | tf_op jit(solution)/shard_map/ppermute | solution.py:317
  7.2 9.5 %collective-permute-start.1 = (f32[184,256]{1,0:T(8,128)S(1)}, f32[184,256]{1,0:T(8,128)S(1)}, u32[]{:S(2)}, u32[]{:S(2)}) collective-permute-start(f32[184,256]{1,0:T(8,128)S(1)} %get-tuple-element.28.fields), channel_id=1, source_target_pairs={{9,1},{11,3},{13,5},{15,7},{0,8},{17,9},{2,10},{19,11},{4,12},{21,... | collective-permute-start | bytes 565256 | tf_op jit(solution)/shard_map/ppermute | solution.py:317
  10.7 11.2 %all-to-all-start = ((f32[8,32,128]{2,1,0:T(8,128)}), f32[8,32,128]{2,1,0:T(8,128)S(1)}, u32[]{:S(2)}, u32[]{:S(2)}) async-start(f32[8,32,128]{2,1,0:T(8,128)} %get-tuple-element.33), calls=%async_computation | async-start | bytes 262144 | tf_op jit(solution)/shard_map/all_to_all | solution.py:304
  17.5 4.8 %collective-permute-start.2 = (f32[184,256]{1,0:T(8,128)}, f32[184,256]{1,0:T(8,128)S(1)}, u32[]{:S(2)}, u32[]{:S(2)}) collective-permute-start(f32[184,256]{1,0:T(8,128)} %get-tuple-element.32), channel_id=1, source_target_pairs={{0,1},{1,0},{2,3},{3,2},{4,5},{5,4},{6,7},{7,6},{8,9},{9,8},{10,11... | collective-permute-start | bytes 565256 | tf_op jit(solution)/shard_map/ppermute | solution.py:320
  23.8 1.6 %collective-permute-start.3 = (f32[90,1,128]{2,1,0:T(1,128)S(1)}, f32[90,1,128]{2,1,0:T(1,128)S(1)}, u32[]{:S(2)}, u32[]{:S(2)}) collective-permute-start(f32[90,1,128]{2,1,0:T(1,128)S(1)} %get-tuple-element.47), channel_id=1, source_target_pairs={{0,1},{1,0},{2,3},{3,2},{4,5},{5,4},{6,7},{7,6},{8,9},{9,8},{10,11... | collective-permute-start | bytes 138248 | tf_op jit(solution)/shard_map/ppermute | solution.py:320
  25.4 4.1 %collective-permute-start.4 = (f32[90,1,128]{2,1,0:T(1,128)S(1)}, f32[90,1,128]{2,1,0:T(1,128)S(1)}, u32[]{:S(2)}, u32[]{:S(2)}) collective-permute-start(f32[90,1,128]{2,1,0:T(1,128)S(1)} %add.6), channel_id=1, source_target_pairs={{0,2},{1,3},{2,0},{3,1},{4,6},{5,7},{6,4},{7,5},{8,10},{9,11},{10,... | collective-permute-start | bytes 138248 | tf_op jit(solution)/shard_map/ppermute | solution.py:320
  29.6 1.3 %collective-permute-start.5 = (f32[90,1,128]{2,1,0:T(1,128)S(1)}, f32[90,1,128]{2,1,0:T(1,128)S(1)}, u32[]{:S(2)}, u32[]{:S(2)}) collective-permute-start(f32[90,1,128]{2,1,0:T(1,128)S(1)} %add.7.piece), channel_id=1, source_target_pairs={{0,1},{1,0},{2,3},{3,2},{4,5},{5,4},{6,7},{7,6},{8,9},{9,8},{10,11... | collective-permute-start | bytes 138248 | tf_op jit(solution)/shard_map/ppermute | solution.py:320
